TPU v7x, 32 devices: a whole 2x2x4 slice. The times are simulated.
32 devices in a mesh: dp: 8 (over z, y), mp: 4 (over x, core).
Axes of the slice: x: 2, y: 2, z: 4, core: 2. Of those that a mesh axis runs over, the one named last changes fastest.
Arguments:
- tokens: bfloat16 [16384, 768], P(('dp', 'mp')), may hold values from -6 to 6
- doc_lengths: int32 [8, 4], P('dp'), may hold values from 1 to 1024, 1792 in all within a row
- attn_gain: float32 [768], replicated, may hold values from 0.5 to 1.5
- attn_shift: float32 [768], replicated, may hold values from -1.75 to 1.75
- query_weight: bfloat16 [768, 768], P(None, 'mp'), may hold values from -0.21875 to 0.21875
- query_bias: float32 [768], P('mp'), may hold values from -1.75 to 1.75
- key_weight: bfloat16 [768, 64], replicated, may hold values from -0.21875 to 0.21875
- key_bias: float32 [64], replicated, may hold values from -3 to 3
- value_weight: bfloat16 [768, 64], replicated, may hold values from -0.21875 to 0.21875
- value_bias: float32 [64], replicated, may hold values from -1.75 to 1.75
- out_weight: bfloat16 [768, 768], P('mp'), may hold values from -0.875 to 0.875
- out_bias: float32 [768], replicated, may hold values from -1.75 to 1.75
- mlp_gain: float32 [768], replicated, may hold values from 0.5 to 1.5
- mlp_shift: float32 [768], replicated, may hold values from -1.75 to 1.75
- up_weight: bfloat16 [768, 3072], P(None, 'mp'), may hold values from -0.21875 to 0.21875
- up_bias: float32 [3072], P('mp'), may hold values from -1.75 to 1.75
- down_weight: bfloat16 [3072, 768], P('mp'), may hold values from -0.21875 to 0.21875
- down_bias: float32 [768], replicated, may hold values from -1.75 to 1.75
- out_grad: bfloat16 [16384, 768], P(('dp', 'mp')), may hold values from -6 to 6
Outputs:
- block_out: bfloat16 [16384, 768], P(('dp', 'mp'))
- input_grad: bfloat16 [16384, 768], P(('dp', 'mp'))
- attn_gain_grad: float32 [768], replicated
- attn_shift_grad: float32 [768], replicated
- query_weight_grad: float32 [768, 768], P(None, 'mp')
- query_bias_grad: float32 [768], P('mp')
- key_weight_grad: float32 [768, 64], replicated
- key_bias_grad: float32 [64], replicated
- value_weight_grad: float32 [768, 64], replicated
- value_bias_grad: float32 [64], replicated
- out_weight_grad: float32 [768, 768], P('mp')
- out_bias_grad: float32 [768], replicated
- mlp_gain_grad: float32 [768], replicated
- mlp_shift_grad: float32 [768], replicated
- up_weight_grad: float32 [768, 3072], P(None, 'mp')
- up_bias_grad: float32 [3072], P('mp')
- down_weight_grad: float32 [3072, 768], P('mp')
- down_bias_grad: float32 [768], replicated
All inputs are finite; a program needn't handle non-finite values.
Results may differ from a plain program's by a relative error of at most 0.02.
Values may be sent and summed in bfloat16 or wider, within the bound.
A program may use at most 128 MiB of HBM per device.

v0:
```python
from functools import partial
import jax
import jax.numpy as jnp
from jax import lax
from jax.sharding import PartitionSpec as P

HD = 64
ROT = 16
SLOT = 2048
DOCS = 4
epsilon = 1e-05


def normalize(values):
    average = jnp.mean(values, axis=-1, keepdims=True)
    centered = values - average
    inv_std = lax.rsqrt(jnp.mean(centered * centered, axis=-1, keepdims=True) + epsilon)
    return (centered * inv_std, inv_std)


def rotate(values, cos_table, sine_table):
    half_rot = ROT // 2
    lower_part = values[..., :half_rot]
    upper_part = values[..., half_rot:ROT]
    return jnp.concatenate(
        [
            lower_part * cos_table - upper_part * sine_table,
            upper_part * cos_table + lower_part * sine_table,
            values[..., ROT:],
        ],
        axis=-1,
    )


def row_layout(lengths):
    slot_index = jnp.arange(SLOT, dtype=jnp.int32)
    doc_ends = jnp.cumsum(lengths, axis=-1)
    doc_starts = doc_ends - lengths
    segment = jnp.sum((slot_index[:, None] >= doc_ends[..., None, :]).astype(jnp.int32), axis=-1)
    doc_begins = jnp.concatenate([doc_starts, doc_ends[..., -1:]], axis=-1)
    labels = jnp.arange(DOCS + 1, dtype=jnp.int32)
    picked = jnp.sum(jnp.where(segment[..., None] == labels, doc_begins[..., None, :], 0), axis=-1)
    return (segment, slot_index - picked)


def angles(position):
    half_rot = ROT // 2
    frequency = 10000.0 ** (-(2.0 * jnp.arange(half_rot, dtype=jnp.float32)) / ROT)
    angle_grid = position.astype(jnp.float32)[..., None] * frequency
    return (jnp.cos(angle_grid), jnp.sin(angle_grid))


def inner_rows(left, right):
    return lax.dot_general(
        left, right, (((0,), (0,)), ((), ())), preferred_element_type=jnp.float32
    )


def times_transposed(left, right):
    return lax.dot_general(
        left, right, (((1,), (1,)), ((), ())), preferred_element_type=jnp.float32
    )


def block_scores(query_block, key_row, seg_row, first_row):
    block_rows = query_block.shape[0]
    scores = jnp.einsum(
        "bhe,ke->hbk", query_block, key_row, preferred_element_type=jnp.float32
    ) * HD ** (-0.5)
    query_index = first_row + jnp.arange(block_rows, dtype=jnp.int32)
    key_index = jnp.arange(SLOT, dtype=jnp.int32)
    seg_rows = lax.dynamic_slice_in_dim(seg_row, first_row, block_rows)
    allowed = (seg_rows[:, None] == seg_row[None, :]) & (key_index[None, :] <= query_index[:, None])
    return (scores, allowed)


def attend_forward(queries, key_rows, value_rows, segment):
    total_rows, heads = (queries.shape[0], queries.shape[1])
    groups = total_rows // SLOT
    block_rows = min(512, SLOT)
    block_count = SLOT // block_rows
    key_groups = key_rows.reshape(groups, SLOT, HD)
    value_groups = value_rows.reshape(groups, SLOT, HD)

    def one_block(block_item):
        query_block, item_index = block_item
        row_index = item_index // block_count
        first_row = item_index % block_count * block_rows
        key_row = lax.dynamic_index_in_dim(key_groups, row_index, 0, keepdims=False)
        value_row = lax.dynamic_index_in_dim(value_groups, row_index, 0, keepdims=False)
        seg_row = lax.dynamic_index_in_dim(segment, row_index, 0, keepdims=False)
        scores, allowed = block_scores(query_block, key_row, seg_row, first_row)
        scores = jnp.where(allowed[None], scores, -1e30)
        peak = jnp.max(scores, axis=-1, keepdims=True)
        expo = jnp.exp(scores - peak)
        totals = jnp.sum(expo, axis=-1, keepdims=True)
        probs_low = (expo / totals).astype(jnp.bfloat16)
        context = jnp.einsum(
            "hbk,ke->bhe", probs_low, value_row, preferred_element_type=jnp.float32
        )
        return (context, (peak + jnp.log(totals))[..., 0])

    item_list = jnp.arange(groups * block_count, dtype=jnp.int32)
    context, summary = lax.map(
        one_block, (queries.reshape(groups * block_count, block_rows, heads, HD), item_list)
    )
    return (context.reshape(total_rows, heads * HD), summary)


def attend_backward(queries, key_rows, value_rows, segment, summary, context_grad):
    total_rows, heads = (queries.shape[0], queries.shape[1])
    groups = total_rows // SLOT
    block_rows = min(512, SLOT)
    block_count = SLOT // block_rows
    key_groups = key_rows.reshape(groups, SLOT, HD)
    value_groups = value_rows.reshape(groups, SLOT, HD)

    def one_block(block_item):
        query_block, grad_block, summary_block, item_index = block_item
        row_index = item_index // block_count
        first_row = item_index % block_count * block_rows
        key_row = lax.dynamic_index_in_dim(key_groups, row_index, 0, keepdims=False)
        value_row = lax.dynamic_index_in_dim(value_groups, row_index, 0, keepdims=False)
        seg_row = lax.dynamic_index_in_dim(segment, row_index, 0, keepdims=False)
        scores, allowed = block_scores(query_block, key_row, seg_row, first_row)
        probs = jnp.where(allowed[None], jnp.exp(scores - summary_block[..., None]), 0.0)
        probs_low = probs.astype(jnp.bfloat16)
        prob_grad = jnp.einsum(
            "bhe,ke->hbk", grad_block, value_row, preferred_element_type=jnp.float32
        )
        delta = jnp.sum(probs * prob_grad, axis=-1, keepdims=True)
        score_grad = (probs * (prob_grad - delta)).astype(jnp.bfloat16)
        query_part = jnp.einsum(
            "hbk,ke->bhe", score_grad, key_row, preferred_element_type=jnp.float32
        ) * HD ** (-0.5)
        key_part = jnp.einsum(
            "hbk,bhe->ke", score_grad, query_block, preferred_element_type=jnp.float32
        ) * HD ** (-0.5)
        value_part = jnp.einsum(
            "hbk,bhe->ke", probs_low, grad_block, preferred_element_type=jnp.float32
        )
        return (query_part, key_part, value_part)

    item_list = jnp.arange(groups * block_count, dtype=jnp.int32)
    query_part, key_part, value_part = lax.map(
        one_block,
        (
            queries.reshape(groups * block_count, block_rows, heads, HD),
            context_grad.reshape(groups * block_count, block_rows, heads, HD),
            summary,
            item_list,
        ),
    )
    key_grad = jnp.sum(key_part.reshape(groups, block_count, SLOT, HD), axis=1).reshape(
        total_rows, HD
    )
    value_grad = jnp.sum(value_part.reshape(groups, block_count, SLOT, HD), axis=1).reshape(
        total_rows, HD
    )
    return (query_part.reshape(total_rows, heads, HD), key_grad, value_grad)


def forward_local(gathered, segment, cos_table, sine_table, local_weights):
    (
        attn_gain,
        attn_shift,
        query_weight,
        query_bias,
        key_weight,
        key_bias,
        value_weight,
        value_bias,
        mlp_gain,
        mlp_shift,
        up_weight,
        up_bias,
    ) = local_weights
    total_rows = gathered.shape[0]
    heads = query_weight.shape[1] // HD
    normed, unused_std = normalize(gathered.astype(jnp.float32))
    attn_in = (normed * attn_gain + attn_shift).astype(jnp.bfloat16)
    mlp_in = (normed * mlp_gain + mlp_shift).astype(jnp.bfloat16)
    queries = jnp.dot(attn_in, query_weight, preferred_element_type=jnp.float32) + query_bias
    queries = rotate(
        queries.reshape(total_rows, heads, HD), cos_table[:, None, :], sine_table[:, None, :]
    ).astype(jnp.bfloat16)
    key_value = jnp.dot(
        attn_in,
        jnp.concatenate([key_weight, value_weight], axis=1),
        preferred_element_type=jnp.float32,
    )
    key_value = key_value + jnp.concatenate([key_bias, value_bias])
    key_rows = rotate(key_value[:, :HD], cos_table, sine_table).astype(jnp.bfloat16)
    value_rows = key_value[:, HD:].astype(jnp.bfloat16)
    context, summary = attend_forward(queries, key_rows, value_rows, segment)
    context = context.astype(jnp.bfloat16)
    hidden_pre = jnp.dot(mlp_in, up_weight, preferred_element_type=jnp.float32) + up_bias
    hidden = jax.nn.gelu(hidden_pre, approximate=False).astype(jnp.bfloat16)
    return (
        attn_in,
        mlp_in,
        queries,
        key_rows,
        value_rows,
        context,
        summary,
        hidden_pre,
        hidden,
        normed,
    )


def per_device(
    tokens,
    doc_lengths,
    attn_gain,
    attn_shift,
    query_weight,
    query_bias,
    key_weight,
    key_bias,
    value_weight,
    value_bias,
    out_weight,
    out_bias,
    mlp_gain,
    mlp_shift,
    up_weight,
    up_bias,
    down_weight,
    down_bias,
    out_grad,
):
    shard_rows = tokens.shape[0]
    my_first = lax.axis_index("mp") * shard_rows
    segment, position = row_layout(doc_lengths)
    cos_table, sine_table = angles(position.reshape(-1))
    shard_valid = lax.dynamic_slice_in_dim(segment.reshape(-1), my_first, shard_rows) < DOCS
    local_weights = (
        attn_gain,
        attn_shift,
        query_weight,
        query_bias,
        key_weight,
        key_bias,
        value_weight,
        value_bias,
        mlp_gain,
        mlp_shift,
        up_weight,
        up_bias,
    )
    gathered = lax.all_gather(tokens, "mp", axis=0, tiled=True)
    kept = forward_local(gathered, segment, cos_table, sine_table, local_weights)
    context_fwd, hidden_fwd = (kept[5], kept[8])
    branch_sum = lax.psum_scatter(
        jnp.dot(context_fwd, out_weight, preferred_element_type=jnp.float32)
        + jnp.dot(hidden_fwd, down_weight, preferred_element_type=jnp.float32),
        "mp",
        scatter_dimension=0,
        tiled=True,
    )
    token_values = tokens.astype(jnp.float32)
    block_out = (token_values + branch_sum + out_bias + down_bias).astype(jnp.bfloat16)
    grad_shard = out_grad * shard_valid[:, None].astype(jnp.bfloat16)
    regathered = lax.all_gather(tokens, "mp", axis=0, tiled=True)
    kept = forward_local(regathered, segment, cos_table, sine_table, local_weights)
    (
        attn_in,
        mlp_in,
        queries,
        key_rows,
        value_rows,
        context,
        summary,
        hidden_pre,
        hidden,
        normed_all,
    ) = kept
    grad_rows = lax.all_gather(grad_shard, "mp", axis=0, tiled=True)
    out_weight_grad = inner_rows(context, grad_rows)
    down_weight_grad = inner_rows(hidden, grad_rows)
    bias_grad = jnp.sum(grad_shard, axis=0, dtype=jnp.float32)
    context_grad = times_transposed(grad_rows, out_weight).astype(jnp.bfloat16)
    hidden_grad = times_transposed(grad_rows, down_weight)
    unused_out, gelu_pull = jax.vjp(partial(jax.nn.gelu, approximate=False), hidden_pre)
    pre_grad = gelu_pull(hidden_grad)[0].astype(jnp.bfloat16)
    up_weight_grad = inner_rows(mlp_in, pre_grad)
    up_bias_grad = jnp.sum(pre_grad, axis=0, dtype=jnp.float32)
    mlp_part = times_transposed(pre_grad, up_weight)
    query_grad, key_part, value_part = attend_backward(
        queries, key_rows, value_rows, segment, summary, context_grad
    )
    total_rows = query_grad.shape[0]
    query_grad = (
        rotate(query_grad, cos_table[:, None, :], -sine_table[:, None, :])
        .reshape(total_rows, -1)
        .astype(jnp.bfloat16)
    )
    key_part = rotate(key_part, cos_table, -sine_table)
    query_weight_grad = inner_rows(attn_in, query_grad)
    query_bias_grad = jnp.sum(query_grad, axis=0, dtype=jnp.float32)
    attn_part = times_transposed(query_grad, query_weight)
    normed, inv_std = normalize(token_values)
    attn_rows = lax.dynamic_slice_in_dim(attn_in, my_first, shard_rows)
    attn_grad, mlp_grad, key_grad, value_grad = (
        lax.psum_scatter(attn_part, "mp", scatter_dimension=0, tiled=True),
        lax.psum_scatter(mlp_part, "mp", scatter_dimension=0, tiled=True),
        lax.psum_scatter(key_part, "mp", scatter_dimension=0, tiled=True),
        lax.psum_scatter(value_part, "mp", scatter_dimension=0, tiled=True),
    )
    key_low = key_grad.astype(jnp.bfloat16)
    value_low = value_grad.astype(jnp.bfloat16)
    attn_grad = (
        attn_grad
        + times_transposed(key_low, key_weight)
        + times_transposed(value_low, value_weight)
    )
    attn_gain_grad = jnp.sum(attn_grad * normed, axis=0)
    attn_shift_grad = jnp.sum(attn_grad, axis=0)
    mlp_gain_grad = jnp.sum(mlp_grad * normed, axis=0)
    mlp_shift_grad = jnp.sum(mlp_grad, axis=0)
    normed_grad = attn_grad * attn_gain + mlp_grad * mlp_gain
    key_weight_grad = inner_rows(attn_rows, key_low)
    key_bias_grad = jnp.sum(key_low, axis=0, dtype=jnp.float32)
    value_weight_grad = inner_rows(attn_rows, value_low)
    value_bias_grad = jnp.sum(value_low, axis=0, dtype=jnp.float32)
    input_grad = inv_std * (
        normed_grad
        - jnp.mean(normed_grad, axis=-1, keepdims=True)
        - normed * jnp.mean(normed_grad * normed, axis=-1, keepdims=True)
    )
    input_grad = (input_grad + grad_shard.astype(jnp.float32)).astype(jnp.bfloat16)
    (
        key_weight_grad,
        key_bias_grad,
        value_weight_grad,
        value_bias_grad,
        attn_gain_grad,
        attn_shift_grad,
        mlp_gain_grad,
        mlp_shift_grad,
        bias_grad,
    ) = lax.psum(
        (
            key_weight_grad,
            key_bias_grad,
            value_weight_grad,
            value_bias_grad,
            attn_gain_grad,
            attn_shift_grad,
            mlp_gain_grad,
            mlp_shift_grad,
            bias_grad,
        ),
        ("dp", "mp"),
    )
    (
        query_weight_grad,
        query_bias_grad,
        out_weight_grad,
        up_weight_grad,
        up_bias_grad,
        down_weight_grad,
    ) = lax.psum(
        (
            query_weight_grad,
            query_bias_grad,
            out_weight_grad,
            up_weight_grad,
            up_bias_grad,
            down_weight_grad,
        ),
        "dp",
    )
    return (
        block_out,
        input_grad,
        attn_gain_grad,
        attn_shift_grad,
        query_weight_grad,
        query_bias_grad,
        key_weight_grad,
        key_bias_grad,
        value_weight_grad,
        value_bias_grad,
        out_weight_grad,
        bias_grad,
        mlp_gain_grad,
        mlp_shift_grad,
        up_weight_grad,
        up_bias_grad,
        down_weight_grad,
        bias_grad,
    )


def solution(mesh):
    placed = (
        P(("dp", "mp"), None),
        P("dp", None),
        P(),
        P(),
        P(None, "mp"),
        P("mp"),
        P(),
        P(),
        P(),
        P(),
        P("mp", None),
        P(),
        P(),
        P(),
        P(None, "mp"),
        P("mp"),
        P("mp", None),
        P(),
        P(("dp", "mp"), None),
    )
    return jax.shard_map(
        per_device,
        mesh=mesh,
        in_specs=placed,
        out_specs=(
            P(("dp", "mp"), None),
            P(("dp", "mp"), None),
            P(),
            P(),
            P(None, "mp"),
            P("mp"),
            P(),
            P(),
            P(),
            P(),
            P("mp", None),
            P(),
            P(),
            P(),
            P(None, "mp"),
            P("mp"),
            P("mp", None),
            P(),
        ),
        check_vma=False,
    )
```

profile of v0, /device:TPU:0, one launch (start us, length us, event | category | flops | bytes accessed | tf_op | source)
XLA Modules:
  0.0 958.1 jit_solution(4647311742938053690)
XLA Ops:
  14.9 26.0 %all-gather.3.cloned.1.call-done = bf16[2048,768]{1,0:T(8,128)(2,1)} async-done(((bf16[512,768]{1,0:T(8,128)(2,1)}), bf16[2048,768]{1,0:T(8,128)(2,1)}) %all-gather.3.cloned.1.call-update) | async-done | bytes 3145744 | tf_op jit(solution)/shard_map/all_gather | solution.py:253
  53.2 96.5 %while.43 = (s32[]{:T(128)}, bf16[4,512,3,64]{1,3,2,0:T(8,128)(2,1)S(1)}, f32[4,3,512]{2,1,0:T(4,128)S(1)}, s32[4]{0:T(128)S(1)}, s32[1,2048]{1,0:T(1,128)S(1)},...) while((s32[]{:T(128)}, ...), condition=%wide.region_15.16_spmd, body=%wide.region_12.15_spmd.sunk | while | flops 846199808 | bytes 43135804 | solution.py:104
  56.9 6.8 bitcast_reduce_fusion.3
  63.8 6.8 fusion.236
  70.6 6.7 fusion.237
  81.1 6.8 bitcast_reduce_fusion.3
  87.9 6.8 fusion.236
  94.7 6.7 fusion.237
  105.2 6.8 bitcast_reduce_fusion.3
  112.0 6.8 fusion.236
  118.8 6.7 fusion.237
  129.3 6.8 bitcast_reduce_fusion.3
  136.2 6.8 fusion.236
  142.9 6.7 fusion.237
  159.1 181.0 %while.44 = (s32[]{:T(128)}, f32[4,512,3,64]{1,0,3,2:T(4,128)}, f32[4,2048,64]{1,2,0:T(8,128)}, f32[4,2048,64]{1,2,0:T(8,128)}, s32[4]{0:T(128)S(1)}, /*index=5*...) while((s32[]{:T(128)}, f32[4,512,3,64]{1,0,3,2:T(4,128)}, ...), condition=%wide.region_18.19_spmd, body=%wide.region_16.18_spmd.sunk | while | flops 2063825920 | bytes 182910384 | solution.py:145
  167.0 6.0 fusion.248
  182.8 8.6 dynamic_update_slice.55
  191.4 4.9 fusion.251
  196.3 8.3 fusion.252
  212.2 6.0 fusion.248
  228.0 8.6 dynamic_update_slice.55
  236.6 4.9 fusion.251
  241.5 8.3 fusion.252
  257.3 6.0 fusion.248
  273.1 8.6 dynamic_update_slice.55
  281.7 4.9 fusion.251
  286.7 8.3 fusion.252
  302.5 6.0 fusion.248
  318.3 8.6 dynamic_update_slice.55
  331.8 8.3 fusion.252
  358.0 85.6 %while.42 = (s32[]{:T(128)}, bf16[4,512,3,64]{1,3,2,0:T(8,128)(2,1)}, s32[4]{0:T(128)S(1)}, s32[1,2048]{1,0:T(1,128)S(1)}, bf16[4,512,3,64]{1,3,2,0:T(8,128)(2,1...) while((s32[]{:T(128)}, ...), condition=%wide.region_8.9_spmd, body=%wide.region_5.8_spmd.sunk | while | flops 827329024 | bytes 28409132 | solution.py:104
  361.8 10.0 %fusion.232 = (f32[3,512]{1,0:T(4,128)S(1)}, f32[3,512,2048]{2,1,0:T(8,128)}) fusion(pred[512,2048]{1,0:T(8,128)(4,1)S(1)} %fusion.231, bf16[1,2048,64]{1,2,0:T(8,128)(2,1)S(1)} %get-tuple-element.756, bf16[4,512,3,64]{1,3,2,0:T(8,128)(2,1)} %get-tuple-element.755, s32[]{:T(128)} %get-tuple-element.738), kind=kOutput, calls=%fused_computation.219.clone.1 | convolution fusion | flops 415238144 | bytes 14096896 | tf_op jit(solution)/shard_map/while/body/eval_jaxpr/sub | solution.py:95
  371.8 7.6 fusion.233
  383.1 10.0 %fusion.232 = (f32[3,512]{1,0:T(4,128)S(1)}, f32[3,512,2048]{2,1,0:T(8,128)}) fusion(pred[512,2048]{1,0:T(8,128)(4,1)S(1)} %fusion.231, bf16[1,2048,64]{1,2,0:T(8,128)(2,1)S(1)} %get-tuple-element.756, bf16[4,512,3,64]{1,3,2,0:T(8,128)(2,1)} %get-tuple-element.755, s32[]{:T(128)} %get-tuple-element.738), kind=kOutput, calls=%fused_computation.219.clone.1 | convolution fusion | flops 415238144 | bytes 14096896 | tf_op jit(solution)/shard_map/while/body/eval_jaxpr/sub | solution.py:95
  393.2 7.6 fusion.233
  404.5 10.6 %fusion.232 = (f32[3,512]{1,0:T(4,128)S(1)}, f32[3,512,2048]{2,1,0:T(8,128)}) fusion(pred[512,2048]{1,0:T(8,128)(4,1)S(1)} %fusion.231, bf16[1,2048,64]{1,2,0:T(8,128)(2,1)S(1)} %get-tuple-element.756, bf16[4,512,3,64]{1,3,2,0:T(8,128)(2,1)} %get-tuple-element.755, s32[]{:T(128)} %get-tuple-element.738), kind=kOutput, calls=%fused_computation.219.clone.1 | convolution fusion | flops 415238144 | bytes 14096896 | tf_op jit(solution)/shard_map/while/body/eval_jaxpr/sub | solution.py:95
  415.2 7.3 fusion.233
  426.3 10.0 %fusion.232 = (f32[3,512]{1,0:T(4,128)S(1)}, f32[3,512,2048]{2,1,0:T(8,128)}) fusion(pred[512,2048]{1,0:T(8,128)(4,1)S(1)} %fusion.231, bf16[1,2048,64]{1,2,0:T(8,128)(2,1)S(1)} %get-tuple-element.756, bf16[4,512,3,64]{1,3,2,0:T(8,128)(2,1)} %get-tuple-element.755, s32[]{:T(128)} %get-tuple-element.738), kind=kOutput, calls=%fused_computation.219.clone.1 | convolution fusion | flops 415238144 | bytes 14096896 | tf_op jit(solution)/shard_map/while/body/eval_jaxpr/sub | solution.py:95
  436.3 7.3 fusion.233
  445.6 5.2 fusion.154
  450.9 17.9 %convert_reduce_fusion.1 = (f32[768]{0:T(1024)S(1)}, bf16[2048,768]{1,0:T(8,128)(2,1)}, f32[2048,768]{1,0:T(8,128)S(1)}) fusion(f32[2048,768]{1,0:T(8,128)S(1)} %fusion.154, f32[768]{0:T(1024)S(1)} %copy-done.41, bf16[2048,768]{1,0:T(8,128)(2,1)S(1)} %copy-done.11, bf16[768,768]{1,0:T(8,128)(2,1)S(1)} %copy-done), kind=kOutput, calls=%fused_computation.108 | convolution fusion | flops 2533883136 | bytes 20060160 | tf_op jit(solution)/shard_map/dot_general | solution.py:60
  477.6 7.5 fusion.172
  509.5 21.8 %all-reduce.2 = (f32[192]{0:T(256)}, f32[768]{0:T(1024)}) all-reduce(f32[192]{0:T(256)S(1)} %reduce_sum.233, f32[768]{0:T(1024)S(1)} %get-tuple-element.519), channel_id=1, replica_groups=mesh['dp'=8,'mp'=4] {'dp'}, use_global_device_ids=true, to_apply=%region_33.34 | all-reduce | flops 960 | bytes 7680 | tf_op jit(solution)/shard_map/psum | solution.py:365
  534.6 60.9 %reduce-scatter.14.cloned.1.call-done = f32[512,768]{1,0:T(8,128)} async-done(((f32[2048,768]{1,0:T(8,128)}), f32[512,768]{1,0:T(8,128)}) %reduce-scatter.14.cloned.1.call-update) | async-done | bytes 1572880 | tf_op jit(solution)/shard_map/reduce_scatter | solution.py:308
  595.5 5.6 fusion.156
  601.1 40.1 %all-reduce = (f32[768]{0:T(1024)}, f32[768]{0:T(1024)}, f32[64]{0:T(128)}, f32[64]{0:T(128)}, f32[768]{0:T(1024)S(1)}, /*index=5*/f32[768]{0:T(1024)}, f32[768]{0:T(1024)}) all-reduce(f32[768]{0:T(1024)S(1)} %get-tuple-element.536, f32[768]{0:T(1024)S(1)} %get-tuple-element.537, ...), channel_id=1, replica_groups=mesh['dp'=8,'mp'=4] {'dp','mp'}, use_global_device_ids=true, to_apply=%region_28.29 | all-reduce | flops 3968 | bytes 31744 | tf_op jit(solution)/shard_map/psum | solution.py:344
  644.1 87.1 %all-reduce.7.cloned.1.call-done = (f32[768,64]{0,1:T(8,128)}, f32[768,64]{0,1:T(8,128)}) async-done(((f32[768,64]{0,1:T(8,128)}, f32[768,64]{0,1:T(8,128)}), (f32[768,64]{0,1:T(8,128)}, f32[768,64]{0,1:T(8,128)})) %all-reduce.7.cloned.1.call-update) | async-done | bytes 393232 | tf_op jit(solution)/shard_map/psum | solution.py:344
  731.2 207.5 %all-reduce.9.cloned.1.call-done = (f32[768,192]{0,1:T(8,128)}, f32[192,768]{1,0:T(8,128)}, f32[768,768]{1,0:T(8,128)}, f32[768,768]{1,0:T(8,128)}) async-done(((f32[768,192]{0,1:T(8,128)}, f32[192,768]{1,0:T(8,128)}, f32[768,768]{1,0:T(8,128)}, f32[768,768]{1,0:T(8,128)}), (f32[768,192]{0,1:T(8,128)}, f32[192,768]{1,0:T(8,128)}, f32[768,768]{1,0:T(8,128)}, ...) | async-done | bytes 5898256 | tf_op jit(solution)/shard_map/psum | solution.py:365
  (299 shorter events, 180.8 us)
Async XLA Ops:
  7.2 443.7 %copy-start = (bf16[768,768]{1,0:T(8,128)(2,1)S(1)}, bf16[768,768]{1,0:T(8,128)(2,1)}, u32[]{:S(2)}) copy-start(bf16[768,768]{1,0:T(8,128)(2,1)} %param.41) | copy-start | bytes 3538948
  7.2 39.2 %copy-start.36 = (f32[768]{0:T(1024)S(1)}, f32[768]{0:T(1024)}, u32[]{:S(2)}) copy-start(f32[768]{0:T(1024)} %param.27) | copy-start | bytes 9220
  7.2 39.2 %copy-start.40 = (f32[768]{0:T(1024)S(1)}, f32[768]{0:T(1024)}, u32[]{:S(2)}) copy-start(f32[768]{0:T(1024)} %param.28) | copy-start | bytes 9220
  7.2 33.7 %all-gather.3.cloned.1.call-start = ((), (), s32[]{:S(2)}) async-start(), calls=%async_computation.5 | async-start | bytes 3932160 | tf_op jit(solution)/shard_map/all_gather | solution.py:253
  8.0 141.8 %all-gather.5.cloned.1.call-start = ((), (), s32[]{:S(2)}) async-start(), calls=%async_computation.7 | async-start | bytes 3932160 | tf_op jit(solution)/shard_map/all_gather | solution.py:280
  11.9 488.8 %reduce-scatter.10.cloned.1.call-start = ((), (), s32[]{:S(2)}) async-start(), calls=%async_computation.9 | async-start | bytes 655360 | tf_op jit(solution)/shard_map/reduce_scatter | solution.py:309
  13.2 37.3 %copy-start.47 = (f32[8]{0:T(128)}, f32[8]{0:T(128)S(1)}, u32[]{:S(2)}) copy-start(f32[8]{0:T(128)S(1)} %multiply_power_fusion) | copy-start | bytes 100
  14.1 36.4 %copy-start.32 = (f32[2048]{0:T(1024)}, f32[2048]{0:T(1024)S(1)}, u32[]{:S(2)}) copy-start(f32[2048]{0:T(1024)S(1)} %subtract_convert_fusion.1) | copy-start | bytes 24580
  14.9 33.1 %copy-start.24 = (bf16[768,64]{0,1:T(8,128)(2,1)S(1)}, bf16[768,64]{0,1:T(8,128)(2,1)}, u32[]{:S(2)}) copy-start(bf16[768,64]{0,1:T(8,128)(2,1)} %param.33) | copy-start | bytes 294916
  14.9 33.1 %copy-start.26 = (bf16[768,64]{0,1:T(8,128)(2,1)S(1)}, bf16[768,64]{0,1:T(8,128)(2,1)}, u32[]{:S(2)}) copy-start(bf16[768,64]{0,1:T(8,128)(2,1)} %param.31) | copy-start | bytes 294916
  53.1 96.6 %copy-start.28 = (bf16[192,768]{1,0:T(8,128)(2,1)S(1)}, bf16[192,768]{1,0:T(8,128)(2,1)}, u32[]{:S(2)}) copy-start(bf16[192,768]{1,0:T(8,128)(2,1)} %param.35) | copy-start | bytes 884740
  149.7 9.4 copy-start.13
  159.1 182.9 %copy-start.33 = (f32[2048]{0:T(1024)S(1)}, f32[2048]{0:T(1024)}, u32[]{:S(2)}) copy-start(f32[2048]{0:T(1024)} %copy-done.32) | copy-start | bytes 24580
  159.1 182.9 %copy-start.48 = (f32[8]{0:T(128)S(1)}, f32[8]{0:T(128)}, u32[]{:S(2)}) copy-start(f32[8]{0:T(128)} %copy-done.47) | copy-start | bytes 100
  167.0 6.0 copy-start.1
  180.4 16.0 %copy-start.3 = (pred[512,2048]{1,0:T(8,128)(4,1)S(1)}, pred[512,2048]{1,0:T(8,128)(4,1)}, u32[]{:S(2)}) copy-start(pred[512,2048]{1,0:T(8,128)(4,1)} %fusion.247) | copy-start | bytes 3145732 | tf_op jit(solution)/shard_map/while
  212.2 6.0 copy-start.1
  225.5 16.0 %copy-start.3 = (pred[512,2048]{1,0:T(8,128)(4,1)S(1)}, pred[512,2048]{1,0:T(8,128)(4,1)}, u32[]{:S(2)}) copy-start(pred[512,2048]{1,0:T(8,128)(4,1)} %fusion.247) | copy-start | bytes 3145732 | tf_op jit(solution)/shard_map/while
  257.3 6.0 copy-start.1
  270.7 16.0 %copy-start.3 = (pred[512,2048]{1,0:T(8,128)(4,1)S(1)}, pred[512,2048]{1,0:T(8,128)(4,1)}, u32[]{:S(2)}) copy-start(pred[512,2048]{1,0:T(8,128)(4,1)} %fusion.247) | copy-start | bytes 3145732 | tf_op jit(solution)/shard_map/while
  302.5 6.0 copy-start.1
  315.8 16.0 %copy-start.3 = (pred[512,2048]{1,0:T(8,128)(4,1)S(1)}, pred[512,2048]{1,0:T(8,128)(4,1)}, u32[]{:S(2)}) copy-start(pred[512,2048]{1,0:T(8,128)(4,1)} %fusion.247) | copy-start | bytes 3145732 | tf_op jit(solution)/shard_map/while
  340.1 10.4 %copy-start.23 = (f32[2048,8]{0,1:T(8,128)S(1)}, f32[2048,8]{0,1:T(8,128)}, u32[]{:S(2)}) copy-start(f32[2048,8]{0,1:T(8,128)} %copy-done.22) | copy-start | bytes 196612
  341.9 11.4 %copy-start.20 = (bf16[768,192]{0,1:T(8,128)(2,1)S(1)}, bf16[768,192]{0,1:T(8,128)(2,1)}, u32[]{:S(2)}) copy-start(bf16[768,192]{0,1:T(8,128)(2,1)} %param.29) | copy-start | bytes 884740
  343.2 159.7 %reduce-scatter.12.cloned.1.call-start = ((), (), s32[]{:S(2)}) async-start(), calls=%async_computation.10 | async-start | bytes 655360 | tf_op jit(solution)/shard_map/reduce_scatter | solution.py:310
  345.8 187.3 %reduce-scatter.8.cloned.1.call-start = ((), (), s32[]{:S(2)}) async-start(), calls=%async_computation.8 | async-start | bytes 7864320 | tf_op jit(solution)/shard_map/reduce_scatter | solution.py:307
  357.0 177.6 %reduce-scatter.6.cloned.1.call-start = ((), (), s32[]{:S(2)}) async-start(), calls=%async_computation.6 | async-start | bytes 7864320 | tf_op jit(solution)/shard_map/reduce_scatter | solution.py:256
  358.0 87.5 %copy-start.31 = (f32[2048]{0:T(1024)S(1)}, f32[2048]{0:T(1024)}, u32[]{:S(2)}) copy-start(f32[2048]{0:T(1024)} %copy-done.30) | copy-start | bytes 24580
  358.0 87.6 %copy-start.35 = (f32[2048]{0:T(1024)S(1)}, f32[2048]{0:T(1024)}, u32[]{:S(2)}) copy-start(f32[2048]{0:T(1024)} %copy-done.34) | copy-start | bytes 24580
  358.0 87.6 %copy-start.42 = (f32[768]{0:T(1024)S(1)}, f32[768]{0:T(1024)}, u32[]{:S(2)}) copy-start(f32[768]{0:T(1024)} %param.37) | copy-start | bytes 9220
  358.0 87.6 %copy-start.50 = (f32[768]{0:T(1024)S(1)}, f32[768]{0:T(1024)}, u32[]{:S(2)}) copy-start(f32[768]{0:T(1024)} %param.38) | copy-start | bytes 9220
  476.3 119.2 %reduce-scatter.14.cloned.1.call-start = ((), (), s32[]{:S(2)}) async-start(), calls=%async_computation.11 | async-start | bytes 7864320 | tf_op jit(solution)/shard_map/reduce_scatter | solution.py:308
  485.1 246.1 %all-reduce.7.cloned.1.call-start = ((), (), s32[]{:S(2)}) async-start(), calls=%async_computation.12 | async-start | bytes 786432 | tf_op jit(solution)/shard_map/psum | solution.py:344
  485.4 6.4 copy-start.12
  485.5 6.4 copy-start.16
  500.7 8.2 copy-start.7
  505.0 26.3 %copy-start.21 = (f32[512,64]{0,1:T(8,128)S(1)}, f32[512,64]{0,1:T(8,128)}, u32[]{:S(2)}) copy-start(f32[512,64]{0,1:T(8,128)} %reduce-scatter.10.cloned.1.call-done) | copy-start | bytes 393220
  505.0 26.4 %copy-start.18 = (f32[512,64]{0,1:T(8,128)S(1)}, f32[512,64]{0,1:T(8,128)}, u32[]{:S(2)}) copy-start(f32[512,64]{0,1:T(8,128)} %reduce-scatter.12.cloned.1.call-done) | copy-start | bytes 393220
  505.0 26.5 %copy-start.27 = (bf16[768,64]{0,1:T(8,128)(2,1)S(1)}, bf16[768,64]{0,1:T(8,128)(2,1)}, u32[]{:S(2)}) copy-start(bf16[768,64]{0,1:T(8,128)(2,1)} %param.31) | copy-start | bytes 294916
  505.1 433.7 %all-reduce.9.cloned.1.call-start = ((), (), s32[]{:S(2)}) async-start(), calls=%async_computation.13 | async-start | bytes 11796480 | tf_op jit(solution)/shard_map/psum | solution.py:365
  505.1 90.4 %copy-start.25 = (bf16[768,64]{0,1:T(8,128)(2,1)S(1)}, bf16[768,64]{0,1:T(8,128)(2,1)}, u32[]{:S(2)}) copy-start(bf16[768,64]{0,1:T(8,128)(2,1)} %param.33) | copy-start | bytes 294916
  505.1 90.4 %copy-start.37 = (f32[768]{0:T(1024)S(1)}, f32[768]{0:T(1024)}, u32[]{:S(2)}) copy-start(f32[768]{0:T(1024)} %param.27) | copy-start | bytes 9220
  505.1 90.4 %copy-start.43 = (f32[768]{0:T(1024)S(1)}, f32[768]{0:T(1024)}, u32[]{:S(2)}) copy-start(f32[768]{0:T(1024)} %param.42) | copy-start | bytes 9220
  505.2 90.4 %copy-start.44 = (f32[768]{0:T(1024)S(1)}, f32[768]{0:T(1024)}, u32[]{:S(2)}) copy-start(f32[768]{0:T(1024)} %param.36) | copy-start | bytes 9220
  509.0 92.1 %copy-start.38 = (f32[768]{0:T(1024)S(1)}, f32[768]{0:T(1024)}, u32[]{:S(2)}) copy-start(f32[768]{0:T(1024)} %get-tuple-element.524) | copy-start | bytes 9220
  509.0 132.1 %copy-start.10 = (bf16[512,768]{1,0:T(8,128)(2,1)S(1)}, bf16[512,768]{1,0:T(8,128)(2,1)}, u32[]{:S(2)}) copy-start(bf16[512,768]{1,0:T(8,128)(2,1)} %get-tuple-element.525) | copy-start | bytes 2359300
  641.2 310.0 %copy-start.46 = (f32[768]{0:T(1024)}, f32[768]{0:T(1024)S(1)}, u32[]{:S(2)}) copy-start(f32[768]{0:T(1024)S(1)} %get-tuple-element.904) | copy-start | bytes 9220
  938.7 11.0 %copy-start.17 = (f32[768,768]{1,0:T(8,128)S(1)}, f32[768,768]{1,0:T(8,128)}, u32[]{:S(2)}) copy-start(f32[768,768]{1,0:T(8,128)} %get-tuple-element.909) | copy-start | bytes 7077892
  (22 other events, 69.1 us)
Sparse Core Ops, SparseCore 0:
  9.6 31.2 all-gather.2
  43.0 28.5 all-gather.4
  343.3 21.6 reduce-scatter.9
  368.0 21.6 reduce-scatter.11
  392.1 58.4 reduce-scatter.7
  476.5 58.0 reduce-scatter.5
  537.1 58.3 reduce-scatter.13
  603.1 128.1 all-reduce.6
  737.0 201.6 all-reduce.8
where the time goes:
time: 964 us; the launch traced here: 958 us
  waiting for transfers between devices  384 us (40%)
  matrix products  296 us (31%)
  other arithmetic  90.6 us (9%)
  local copies, waits for them, and re-layouts  85.2 us (9%)
  blocking collectives  61.9 us (6%)
  loops' own time  24.6 us (3%)
  between operations  15.1 us (2%)
    psum x1, waiting for transfers between devices, per_device(): lax.psum((query_weight_grad, query_bias_grad, out_weight_grad, up_weight_...  208 us
    psum x1, waiting for transfers between devices, per_device(): lax.psum((key_weight_grad, key_bias_grad, value_weight_grad, value_bias_g...  87.1 us
    reduce_scatter x1, waiting for transfers between devices, per_device(): lax.psum_scatter(mlp_part, 'mp', scatter_dimension=0, tiled=True)  60.9 us
    dot_general x8, matrix products, one_block(): jnp.einsum('hbk,ke->bhe', probs_low, value_row, preferred_element_type=jn...  56.8 us
    sub x4, matrix products, one_block(): expo = jnp.exp(scores - peak)  40.6 us
    dot_general x6, matrix products, times_transposed(): lax.dot_general(left, right, (((1,), (1,)), ((), ())), preferred_element_...  40.4 us
    psum x1, blocking collectives, per_device(): lax.psum((key_weight_grad, key_bias_grad, value_weight_grad, value_bias_g...  40.1 us
    dot_general x8, matrix products, block_scores(): jnp.einsum('bhe,ke->hbk', query_block, key_row, preferred_element_type=jn...  38.3 us
  transfers between devices with their start and end apart: 9, of which 5 were waited for; matrix products, arithmetic and copies ran while one was open for 28% of the time, Pallas kernels for 0%

commit v1 on v0

--- a/solution.py
+++ b/solution.py
@@ -342,18 +342,21 @@
         mlp_shift_grad,
         bias_grad,
     ) = lax.psum(
-        (
-            key_weight_grad,
-            key_bias_grad,
-            value_weight_grad,
-            value_bias_grad,
-            attn_gain_grad,
-            attn_shift_grad,
-            mlp_gain_grad,
-            mlp_shift_grad,
-            bias_grad,
+        lax.psum(
+            (
+                key_weight_grad,
+                key_bias_grad,
+                value_weight_grad,
+                value_bias_grad,
+                attn_gain_grad,
+                attn_shift_grad,
+                mlp_gain_grad,
+                mlp_shift_grad,
+                bias_grad,
+            ),
+            "mp",
         ),
-        ("dp", "mp"),
+        "dp",
     )
     (
         query_weight_grad,

time: 964 us -> 884 us (0.917)
  waiting for transfers between devices: 384 us -> 317 us
  blocking collectives: 61.9 us -> 50.2 us
    psum x1, waiting for transfers between devices: 87.1 us -> 0.02 us  [per_device(): lax.psum((key_weight_grad, key_bias_grad, value_weight_grad, value_bias_g...]
    psum x1, waiting for transfers between devices: 208 us -> 165 us  [per_device(): lax.psum((query_weight_grad, query_bias_grad, out_weight_grad, up_weight_...]
    psum x1, blocking collectives: 40.1 us -> 10.2 us  [per_device(): lax.psum((key_weight_grad, key_bias_grad, value_weight_grad, value_bias_g...]
    reduce_scatter x1, waiting for transfers between devices: 1.49 us -> 29.3 us  [per_device(): lax.psum_scatter(jnp.dot(context_fwd, out_weight, preferred_element_type=...]
    reduce_scatter x1, waiting for transfers between devices: 0.01 us -> 22.6 us  [per_device(): lax.psum_scatter(value_part, 'mp', scatter_dimension=0, tiled=True)]
    psum x1, blocking collectives: 21.8 us -> 40 us  [per_device(): lax.psum(lax.psum((key_weight_grad, key_bias_grad, value_weight_grad, val...]
    reduce_scatter x1, waiting for transfers between devices: 0.01 us -> 12.5 us  [per_device(): lax.psum_scatter(key_part, 'mp', scatter_dimension=0, tiled=True)]
  transfers between devices with their start and end apart: 9 -> 9, of which waited for: 5 -> 6; matrix products, arithmetic and copies ran while one was open for 28% -> 30% of each run, Pallas kernels for 0% -> 0%
where the time goes in v1:
time: 884 us; the launch traced here: 878 us
  waiting for transfers between devices  317 us (36%)
  matrix products  294 us (33%)
  other arithmetic  90.5 us (10%)
  local copies, waits for them, and re-layouts  85.3 us (10%)
  blocking collectives  50.2 us (6%)
  loops' own time  24.6 us (3%)
  between operations  15.1 us (2%)
    psum x1, waiting for transfers between devices, per_device(): lax.psum((query_weight_grad, query_bias_grad, out_weight_grad, up_weight_...  165 us
    reduce_scatter x1, waiting for transfers between devices, per_device(): lax.psum_scatter(mlp_part, 'mp', scatter_dimension=0, tiled=True)  61.1 us
    dot_general x8, matrix products, one_block(): jnp.einsum('hbk,ke->bhe', probs_low, value_row, preferred_element_type=jn...  58 us
    dot_general x6, matrix products, times_transposed(): lax.dot_general(left, right, (((1,), (1,)), ((), ())), preferred_element_...  40.1 us
    psum x1, blocking collectives, per_device(): lax.psum(lax.psum((key_weight_grad, key_bias_grad, value_weight_grad, val...  40 us
    sub x4, matrix products, one_block(): expo = jnp.exp(scores - peak)  39.9 us
    dot_general x8, matrix products, block_scores(): jnp.einsum('bhe,ke->hbk', query_block, key_row, preferred_element_type=jn...  38.3 us
    dynamic_update_slice x8, local copies, waits for them, and re-layouts, attend_forward(): lax.map(one_block, (queries.reshape(groups * block_count, block_rows, hea...  36.1 us
  transfers between devices with their start and end apart: 9, of which 6 were waited for; matrix products, arithmetic and copies ran while one was open for 30% of the time, Pallas kernels for 0%

profile of v1, /device:TPU:0, one launch (start us, length us, event | category | flops | bytes accessed | tf_op | source)
XLA Modules:
  0.0 878.1 jit_solution(11320731077645990109)
XLA Ops:
  14.9 26.0 %all-gather.3.cloned.1.call-done = bf16[2048,768]{1,0:T(8,128)(2,1)} async-done(((bf16[512,768]{1,0:T(8,128)(2,1)}), bf16[2048,768]{1,0:T(8,128)(2,1)}) %all-gather.3.cloned.1.call-update) | async-done | bytes 3145744 | tf_op jit(solution)/shard_map/all_gather | solution.py:253
  53.2 96.5 %while.43 = (s32[]{:T(128)}, bf16[4,512,3,64]{1,3,2,0:T(8,128)(2,1)S(1)}, f32[4,3,512]{2,1,0:T(4,128)S(1)}, s32[4]{0:T(128)S(1)}, s32[1,2048]{1,0:T(1,128)S(1)},...) while((s32[]{:T(128)}, ...), condition=%wide.region_15.16_spmd, body=%wide.region_12.15_spmd.sunk | while | flops 846199808 | bytes 43135804 | solution.py:104
  56.9 6.8 bitcast_reduce_fusion.3
  63.8 6.8 fusion.236
  70.6 6.7 fusion.237
  81.1 6.8 bitcast_reduce_fusion.3
  87.9 6.8 fusion.236
  94.7 6.7 fusion.237
  105.2 6.8 bitcast_reduce_fusion.3
  112.0 6.8 fusion.236
  118.8 6.7 fusion.237
  129.3 6.8 bitcast_reduce_fusion.3
  136.1 6.8 fusion.236
  142.9 6.7 fusion.237
  159.1 181.0 %while.44 = (s32[]{:T(128)}, f32[4,512,3,64]{1,0,3,2:T(4,128)}, f32[4,2048,64]{1,2,0:T(8,128)}, f32[4,2048,64]{1,2,0:T(8,128)}, s32[4]{0:T(128)S(1)}, /*index=5*...) while((s32[]{:T(128)}, f32[4,512,3,64]{1,0,3,2:T(4,128)}, ...), condition=%wide.region_18.19_spmd, body=%wide.region_16.18_spmd.sunk | while | flops 2063825920 | bytes 182910384 | solution.py:145
  167.0 6.0 fusion.248
  182.8 8.6 dynamic_update_slice.55
  196.3 8.3 fusion.252
  212.2 6.0 fusion.248
  228.0 8.6 dynamic_update_slice.55
  241.5 8.3 fusion.252
  257.3 6.0 fusion.248
  273.1 8.6 dynamic_update_slice.55
  281.7 4.9 fusion.251
  286.6 8.3 fusion.252
  302.5 6.0 fusion.248
  318.3 8.6 dynamic_update_slice.55
  331.8 8.3 fusion.252
  352.4 12.5 %reduce-scatter.10.cloned.1.call-done = f32[512,64]{0,1:T(8,128)} async-done(((f32[2048,64]{0,1:T(8,128)}), f32[512,64]{0,1:T(8,128)}) %reduce-scatter.10.cloned.1.call-update) | async-done | bytes 131088 | tf_op jit(solution)/shard_map/reduce_scatter | solution.py:309
  367.1 22.6 %reduce-scatter.12.cloned.1.call-done = f32[512,64]{0,1:T(8,128)} async-done(((f32[2048,64]{0,1:T(8,128)}), f32[512,64]{0,1:T(8,128)}) %reduce-scatter.12.cloned.1.call-update) | async-done | bytes 131088 | tf_op jit(solution)/shard_map/reduce_scatter | solution.py:310
  396.6 86.1 %while.42 = (s32[]{:T(128)}, bf16[4,512,3,64]{1,3,2,0:T(8,128)(2,1)}, s32[4]{0:T(128)S(1)}, s32[1,2048]{1,0:T(1,128)S(1)}, bf16[4,512,3,64]{1,3,2,0:T(8,128)(2,1...) while((s32[]{:T(128)}, ...), condition=%wide.region_8.9_spmd, body=%wide.region_5.8_spmd.sunk | while | flops 827329024 | bytes 28409132 | solution.py:104
  400.4 10.0 %fusion.232 = (f32[3,512]{1,0:T(4,128)S(1)}, f32[3,512,2048]{2,1,0:T(8,128)}) fusion(pred[512,2048]{1,0:T(8,128)(4,1)S(1)} %fusion.231, bf16[1,2048,64]{1,2,0:T(8,128)(2,1)S(1)} %get-tuple-element.765, bf16[4,512,3,64]{1,3,2,0:T(8,128)(2,1)} %get-tuple-element.764, s32[]{:T(128)} %get-tuple-element.747), kind=kOutput, calls=%fused_computation.219.clone.1 | convolution fusion | flops 415238144 | bytes 14096896 | tf_op jit(solution)/shard_map/while/body/eval_jaxpr/sub | solution.py:95
  410.4 7.4 fusion.233
  421.5 10.0 %fusion.232 = (f32[3,512]{1,0:T(4,128)S(1)}, f32[3,512,2048]{2,1,0:T(8,128)}) fusion(pred[512,2048]{1,0:T(8,128)(4,1)S(1)} %fusion.231, bf16[1,2048,64]{1,2,0:T(8,128)(2,1)S(1)} %get-tuple-element.765, bf16[4,512,3,64]{1,3,2,0:T(8,128)(2,1)} %get-tuple-element.764, s32[]{:T(128)} %get-tuple-element.747), kind=kOutput, calls=%fused_computation.219.clone.1 | convolution fusion | flops 415238144 | bytes 14096896 | tf_op jit(solution)/shard_map/while/body/eval_jaxpr/sub | solution.py:95
  431.5 8.9 %fusion.233 = bf16[4,512,3,64]{1,3,2,0:T(8,128)(2,1)} fusion(bf16[4,512,3,64]{1,3,2,0:T(8,128)(2,1)} %get-tuple-element.748, s32[]{:T(128)} %get-tuple-element.747, f32[3,512,2048]{2,1,0:T(8,128)} %get-tuple-element.709, f32[3,512]{1,0:T(4,128)S(1)} %get-tuple-element.710, bf16[1,2048,64]{1,2,0:T(8,128)(2,1)S(1)} %get-tuple-element.766), kind=kOutput, calls=%fused_computation.15.clone.1 | convolution fusion | flops 408944640 | bytes 13244928 | tf_op jit(solution)/shard_map/while/body/eval_jaxpr/hbk,ke->bhe/dot_general | solution.py:98
  444.1 10.0 %fusion.232 = (f32[3,512]{1,0:T(4,128)S(1)}, f32[3,512,2048]{2,1,0:T(8,128)}) fusion(pred[512,2048]{1,0:T(8,128)(4,1)S(1)} %fusion.231, bf16[1,2048,64]{1,2,0:T(8,128)(2,1)S(1)} %get-tuple-element.765, bf16[4,512,3,64]{1,3,2,0:T(8,128)(2,1)} %get-tuple-element.764, s32[]{:T(128)} %get-tuple-element.747), kind=kOutput, calls=%fused_computation.219.clone.1 | convolution fusion | flops 415238144 | bytes 14096896 | tf_op jit(solution)/shard_map/while/body/eval_jaxpr/sub | solution.py:95
  454.1 7.3 fusion.233
  465.2 10.0 %fusion.232 = (f32[3,512]{1,0:T(4,128)S(1)}, f32[3,512,2048]{2,1,0:T(8,128)}) fusion(pred[512,2048]{1,0:T(8,128)(4,1)S(1)} %fusion.231, bf16[1,2048,64]{1,2,0:T(8,128)(2,1)S(1)} %get-tuple-element.765, bf16[4,512,3,64]{1,3,2,0:T(8,128)(2,1)} %get-tuple-element.764, s32[]{:T(128)} %get-tuple-element.747), kind=kOutput, calls=%fused_computation.219.clone.1 | convolution fusion | flops 415238144 | bytes 14096896 | tf_op jit(solution)/shard_map/while/body/eval_jaxpr/sub | solution.py:95
  475.2 7.5 fusion.233
  484.7 5.2 fusion.154
  489.9 17.9 %convert_reduce_fusion.1 = (f32[768]{0:T(1024)S(1)}, bf16[2048,768]{1,0:T(8,128)(2,1)}, f32[2048,768]{1,0:T(8,128)S(1)}) fusion(f32[2048,768]{1,0:T(8,128)S(1)} %fusion.154, f32[768]{0:T(1024)S(1)} %copy-done.41, bf16[2048,768]{1,0:T(8,128)(2,1)S(1)} %copy-done.11, bf16[768,768]{1,0:T(8,128)(2,1)S(1)} %copy-done), kind=kOutput, calls=%fused_computation.108 | convolution fusion | flops 2533883136 | bytes 20060160 | tf_op jit(solution)/shard_map/dot_general | solution.py:60
  516.6 7.2 fusion.172
  544.8 29.3 %reduce-scatter.6.cloned.1.call-done = f32[512,768]{1,0:T(8,128)} async-done(((f32[2048,768]{1,0:T(8,128)}), f32[512,768]{1,0:T(8,128)}) %reduce-scatter.6.cloned.1.call-update) | async-done | bytes 1572880 | tf_op jit(solution)/shard_map/reduce_scatter | solution.py:256
  574.1 61.1 %reduce-scatter.14.cloned.1.call-done = f32[512,768]{1,0:T(8,128)} async-done(((f32[2048,768]{1,0:T(8,128)}), f32[512,768]{1,0:T(8,128)}) %reduce-scatter.14.cloned.1.call-update) | async-done | bytes 1572880 | tf_op jit(solution)/shard_map/reduce_scatter | solution.py:308
  635.2 5.6 fusion.156
  640.7 10.2 %all-reduce.2 = (f32[768]{0:T(1024)S(1)}, f32[768]{0:T(1024)S(1)}, f32[64]{0:T(128)S(1)}, f32[64]{0:T(128)S(1)}, f32[768]{0:T(1024)S(1)}, /*index=5*/f32[768]{0:T(1024)S(1)}, f32[768]{0:T(1024)S(1)}) all-reduce(f32[768]{0:T(1024)S(1)} %get-tuple-element.545, f32[768]{0:T(1024)S(1)} %get-tuple-element.546, ...), channel_id=1, replica_groups=mesh['dp'=8,'mp'=4] {'mp'}, use_global_device_ids=true, to_apply=%region_28.29 | all-reduce | flops 3968 | bytes 31744 | tf_op jit(solution)/shard_map/psum | solution.py:345
  651.0 40.0 %all-reduce = (f32[768]{0:T(1024)}, f32[768]{0:T(1024)}, f32[192]{0:T(256)}, f32[64]{0:T(128)}, f32[64]{0:T(128)}, /*index=5*/f32[768]{0:T(1024)S(1)}, f32[768]{0:T(1024)}, f32[768]{0:T(1024)}, f32[768]{0:T(1024)}) all-reduce(f32[768]{0:T(1024)S(1)} %get-tuple-element.519, ...), channel_id=1, replica_groups=mesh['dp'=8,'mp'=4] {'dp'}, use_global_device_ids=true, to_apply=%region_29.30 | all-reduce | flops 4928 | bytes 39424 | tf_op jit(solution)/shard_map/psum | solution.py:344
  693.9 164.8 %all-reduce.7.cloned.1.call-done = (f32[768,192]{0,1:T(8,128)}, f32[768,64]{0,1:T(8,128)}, f32[768,64]{0,1:T(8,128)}, f32[192,768]{1,0:T(8,128)}, f32[768,768]{1,0:T(8,128)}, /*index=5*/f32[768,768]{1,0:T(8,128)}) async-done(((f32[768,192]{0,1:T(8,128)}, f32[768,64]{0,1:T(8,128)}, f32[768,64]{0,1:T(8,128)}, f32[192,768]{1,0:T(8,128)}, f32[768,768]{1,0:T(8,128)}, /*index=5*/f32[768,768]{1,0:T(8,128)}), ...) | async-done | bytes 6291472 | tf_op jit(solution)/shard_map/psum | solution.py:368
  (299 shorter events, 187.2 us)
Async XLA Ops:
  7.2 482.7 %copy-start = (bf16[768,768]{1,0:T(8,128)(2,1)S(1)}, bf16[768,768]{1,0:T(8,128)(2,1)}, u32[]{:S(2)}) copy-start(bf16[768,768]{1,0:T(8,128)(2,1)} %param.41) | copy-start | bytes 3538948
  7.2 39.2 %copy-start.36 = (f32[768]{0:T(1024)S(1)}, f32[768]{0:T(1024)}, u32[]{:S(2)}) copy-start(f32[768]{0:T(1024)} %param.27) | copy-start | bytes 9220
  7.2 39.2 %copy-start.40 = (f32[768]{0:T(1024)S(1)}, f32[768]{0:T(1024)}, u32[]{:S(2)}) copy-start(f32[768]{0:T(1024)} %param.28) | copy-start | bytes 9220
  7.2 33.7 %all-gather.3.cloned.1.call-start = ((), (), s32[]{:S(2)}) async-start(), calls=%async_computation.5 | async-start | bytes 3932160 | tf_op jit(solution)/shard_map/all_gather | solution.py:253
  8.0 141.7 %all-gather.5.cloned.1.call-start = ((), (), s32[]{:S(2)}) async-start(), calls=%async_computation.7 | async-start | bytes 3932160 | tf_op jit(solution)/shard_map/all_gather | solution.py:280
  11.9 353.0 %reduce-scatter.10.cloned.1.call-start = ((), (), s32[]{:S(2)}) async-start(), calls=%async_computation.9 | async-start | bytes 655360 | tf_op jit(solution)/shard_map/reduce_scatter | solution.py:309
  13.2 37.3 %copy-start.47 = (f32[8]{0:T(128)}, f32[8]{0:T(128)S(1)}, u32[]{:S(2)}) copy-start(f32[8]{0:T(128)S(1)} %multiply_power_fusion) | copy-start | bytes 100
  14.1 36.4 %copy-start.32 = (f32[2048]{0:T(1024)}, f32[2048]{0:T(1024)S(1)}, u32[]{:S(2)}) copy-start(f32[2048]{0:T(1024)S(1)} %subtract_convert_fusion.1) | copy-start | bytes 24580
  14.9 33.1 %copy-start.24 = (bf16[768,64]{0,1:T(8,128)(2,1)S(1)}, bf16[768,64]{0,1:T(8,128)(2,1)}, u32[]{:S(2)}) copy-start(bf16[768,64]{0,1:T(8,128)(2,1)} %param.33) | copy-start | bytes 294916
  14.9 33.1 %copy-start.26 = (bf16[768,64]{0,1:T(8,128)(2,1)S(1)}, bf16[768,64]{0,1:T(8,128)(2,1)}, u32[]{:S(2)}) copy-start(bf16[768,64]{0,1:T(8,128)(2,1)} %param.31) | copy-start | bytes 294916
  40.9 5.5 copy-start.5
  43.4 5.7 copy-start.30
  53.1 96.6 %copy-start.28 = (bf16[192,768]{1,0:T(8,128)(2,1)S(1)}, bf16[192,768]{1,0:T(8,128)(2,1)}, u32[]{:S(2)}) copy-start(bf16[192,768]{1,0:T(8,128)(2,1)} %param.35) | copy-start | bytes 884740
  149.7 9.4 %copy-start.13 = (bf16[4,512,3,64]{1,3,2,0:T(8,128)(2,1)}, bf16[4,512,3,64]{1,3,2,0:T(8,128)(2,1)S(1)}, u32[]{:S(2)}) copy-start(bf16[4,512,3,64]{1,3,2,0:T(8,128)(2,1)S(1)} %get-tuple-element.356) | copy-start | bytes 2359300
  159.1 182.8 %copy-start.33 = (f32[2048]{0:T(1024)S(1)}, f32[2048]{0:T(1024)}, u32[]{:S(2)}) copy-start(f32[2048]{0:T(1024)} %copy-done.32) | copy-start | bytes 24580
  159.1 182.9 %copy-start.48 = (f32[8]{0:T(128)S(1)}, f32[8]{0:T(128)}, u32[]{:S(2)}) copy-start(f32[8]{0:T(128)} %copy-done.47) | copy-start | bytes 100
  167.0 6.0 copy-start.1
  180.4 16.0 %copy-start.3 = (pred[512,2048]{1,0:T(8,128)(4,1)S(1)}, pred[512,2048]{1,0:T(8,128)(4,1)}, u32[]{:S(2)}) copy-start(pred[512,2048]{1,0:T(8,128)(4,1)} %fusion.247) | copy-start | bytes 3145732 | tf_op jit(solution)/shard_map/while
  212.1 6.0 copy-start.1
  225.5 16.0 %copy-start.3 = (pred[512,2048]{1,0:T(8,128)(4,1)S(1)}, pred[512,2048]{1,0:T(8,128)(4,1)}, u32[]{:S(2)}) copy-start(pred[512,2048]{1,0:T(8,128)(4,1)} %fusion.247) | copy-start | bytes 3145732 | tf_op jit(solution)/shard_map/while
  257.3 6.0 copy-start.1
  270.7 16.0 %copy-start.3 = (pred[512,2048]{1,0:T(8,128)(4,1)S(1)}, pred[512,2048]{1,0:T(8,128)(4,1)}, u32[]{:S(2)}) copy-start(pred[512,2048]{1,0:T(8,128)(4,1)} %fusion.247) | copy-start | bytes 3145732 | tf_op jit(solution)/shard_map/while
  302.5 6.0 copy-start.1
  315.8 16.0 %copy-start.3 = (pred[512,2048]{1,0:T(8,128)(4,1)S(1)}, pred[512,2048]{1,0:T(8,128)(4,1)}, u32[]{:S(2)}) copy-start(pred[512,2048]{1,0:T(8,128)(4,1)} %fusion.247) | copy-start | bytes 3145732 | tf_op jit(solution)/shard_map/while
  340.1 10.4 %copy-start.23 = (f32[2048,8]{0,1:T(8,128)S(1)}, f32[2048,8]{0,1:T(8,128)}, u32[]{:S(2)}) copy-start(f32[2048,8]{0,1:T(8,128)} %copy-done.22) | copy-start | bytes 196612
  343.1 48.8 %copy-start.20 = (bf16[768,192]{0,1:T(8,128)(2,1)S(1)}, bf16[768,192]{0,1:T(8,128)(2,1)}, u32[]{:S(2)}) copy-start(bf16[768,192]{0,1:T(8,128)(2,1)} %param.29) | copy-start | bytes 884740
  343.1 46.5 %reduce-scatter.12.cloned.1.call-start = ((), (), s32[]{:S(2)}) async-start(), calls=%async_computation.10 | async-start | bytes 655360 | tf_op jit(solution)/shard_map/reduce_scatter | solution.py:310
  345.7 195.5 %all-reduce.9.cloned.1.call-start = ((), (), s32[]{:S(2)}) async-start(), calls=%async_computation.13 | async-start | bytes 786432 | tf_op jit(solution)/shard_map/psum | solution.py:345
  352.4 43.2 %copy-start.8 = (bf16[2048,3,64]{0,2,1:T(8,128)(2,1)}, bf16[2048,3,64]{0,2,1:T(8,128)(2,1)S(1)}, u32[]{:S(2)}) copy-start(bf16[2048,3,64]{0,2,1:T(8,128)(2,1)S(1)} %get-tuple-element.532) | copy-start | bytes 2359300
  391.8 152.9 %reduce-scatter.8.cloned.1.call-start = ((), (), s32[]{:S(2)}) async-start(), calls=%async_computation.8 | async-start | bytes 7864320 | tf_op jit(solution)/shard_map/reduce_scatter | solution.py:307
  395.6 178.5 %reduce-scatter.6.cloned.1.call-start = ((), (), s32[]{:S(2)}) async-start(), calls=%async_computation.6 | async-start | bytes 7864320 | tf_op jit(solution)/shard_map/reduce_scatter | solution.py:256
  396.6 88.0 %copy-start.31 = (f32[2048]{0:T(1024)S(1)}, f32[2048]{0:T(1024)}, u32[]{:S(2)}) copy-start(f32[2048]{0:T(1024)} %copy-done.30) | copy-start | bytes 24580
  396.6 88.0 %copy-start.35 = (f32[2048]{0:T(1024)S(1)}, f32[2048]{0:T(1024)}, u32[]{:S(2)}) copy-start(f32[2048]{0:T(1024)} %copy-done.34) | copy-start | bytes 24580
  396.6 88.0 %copy-start.42 = (f32[768]{0:T(1024)S(1)}, f32[768]{0:T(1024)}, u32[]{:S(2)}) copy-start(f32[768]{0:T(1024)} %param.37) | copy-start | bytes 9220
  396.6 88.0 %copy-start.50 = (f32[768]{0:T(1024)S(1)}, f32[768]{0:T(1024)}, u32[]{:S(2)}) copy-start(f32[768]{0:T(1024)} %param.38) | copy-start | bytes 9220
  484.6 5.3 copy-start.11
  515.4 119.8 %reduce-scatter.14.cloned.1.call-start = ((), (), s32[]{:S(2)}) async-start(), calls=%async_computation.11 | async-start | bytes 7864320 | tf_op jit(solution)/shard_map/reduce_scatter | solution.py:308
  523.9 334.7 %all-reduce.7.cloned.1.call-start = ((), (), s32[]{:S(2)}) async-start(), calls=%async_computation.12 | async-start | bytes 12582912 | tf_op jit(solution)/shard_map/psum | solution.py:368
  524.2 6.5 copy-start.12
  524.2 8.1 copy-start.16
  541.2 94.0 %copy-start.25 = (bf16[768,64]{0,1:T(8,128)(2,1)S(1)}, bf16[768,64]{0,1:T(8,128)(2,1)}, u32[]{:S(2)}) copy-start(bf16[768,64]{0,1:T(8,128)(2,1)} %param.33) | copy-start | bytes 294916
  541.2 94.0 %copy-start.37 = (f32[768]{0:T(1024)S(1)}, f32[768]{0:T(1024)}, u32[]{:S(2)}) copy-start(f32[768]{0:T(1024)} %param.27) | copy-start | bytes 9220
  541.2 93.9 %copy-start.43 = (f32[768]{0:T(1024)S(1)}, f32[768]{0:T(1024)}, u32[]{:S(2)}) copy-start(f32[768]{0:T(1024)} %param.42) | copy-start | bytes 9220
  541.2 93.9 %copy-start.44 = (f32[768]{0:T(1024)S(1)}, f32[768]{0:T(1024)}, u32[]{:S(2)}) copy-start(f32[768]{0:T(1024)} %param.36) | copy-start | bytes 9220
  542.5 98.2 %copy-start.38 = (f32[768]{0:T(1024)S(1)}, f32[768]{0:T(1024)}, u32[]{:S(2)}) copy-start(f32[768]{0:T(1024)} %get-tuple-element.533) | copy-start | bytes 9220
  542.5 148.5 %copy-start.10 = (bf16[512,768]{1,0:T(8,128)(2,1)S(1)}, bf16[512,768]{1,0:T(8,128)(2,1)}, u32[]{:S(2)}) copy-start(bf16[512,768]{1,0:T(8,128)(2,1)} %get-tuple-element.534) | copy-start | bytes 2359300
  691.0 180.1 %copy-start.46 = (f32[768]{0:T(1024)}, f32[768]{0:T(1024)S(1)}, u32[]{:S(2)}) copy-start(f32[768]{0:T(1024)S(1)} %get-tuple-element.913) | copy-start | bytes 9220
  858.7 11.0 %copy-start.17 = (f32[768,768]{1,0:T(8,128)S(1)}, f32[768,768]{1,0:T(8,128)}, u32[]{:S(2)}) copy-start(f32[768,768]{1,0:T(8,128)} %get-tuple-element.918) | copy-start | bytes 7077892
  (22 other events, 55.8 us)
Sparse Core Ops, SparseCore 0:
  9.6 31.2 all-gather.2
  43.0 28.5 all-gather.4
  343.2 21.6 reduce-scatter.9
  368.0 21.6 reduce-scatter.11
  393.0 32.7 all-reduce.8
  428.3 58.3 reduce-scatter.7
  515.5 58.4 reduce-scatter.5
  576.7 58.3 reduce-scatter.13
  642.1 216.5 all-reduce.6
